TPU v7x, 512 devices: a whole 4x8x8 slice. The times are simulated.
512 devices in a mesh: grp: 8 (over y_lo, x), sub: 64 (over z, y_hi, core).
Axes of the slice: x: 4, y: 8 (y_hi: 4, y_lo: 2; y = y_hi * 2 + y_lo), z: 8, core: 2. Of those that a mesh axis runs over, the one named last changes fastest.
Arguments:
- schur_t: bfloat16 [8, 64, 1024, 1024], P('grp', 'sub')
- neumann_t: bfloat16 [8, 64, 1024, 1024], P('grp', 'sub')
- face_weights: float32 [8, 64, 1024], P('grp', 'sub'), as said below
- coarse_basis: bfloat16 [8, 64, 1024, 24], P('grp', 'sub'), may hold values from -0.375 to 0.375
- coarse_inverse: float32 [8, 768, 768], P('grp', 'sub')
- coarse_number: int32 [8, 1536], P('grp'), may hold values from 0 to 767, as said below
- loads: bfloat16 [8, 64, 1024, 128], P('grp', 'sub'), may hold values from -6 to 6
- iterate: bfloat16 [8, 64, 1024, 128], P('grp', 'sub'), as said below
Outputs:
- iterate_out: bfloat16 [8, 64, 1024, 128], P('grp', 'sub')
Inputs may be any that keep to these rules, and one draw needn't show every extreme that they name: `face_weights`: the weights of an unknown and of its partner unknown on the face it shares sum to one. `coarse_number`: each value appears exactly twice in each group's row. `iterate`: equal on the two copies of each shared unknown.
All inputs are finite; a program needn't handle non-finite values.
Results may differ from a plain program's by a relative error of at most 0.0051.
Values sent between devices are 32-bit elements; how exact they have to be, the bound alone decides.
A program may use at most 64 MiB of HBM per device.

v0:
```python
import jax
import jax.numpy as jnp
from jax import lax
from jax.sharding import PartitionSpec as P

ITERS = 3


def extended(array, sides, width):
    for axis, dim in sides:
        devices, length = (lax.axis_size(axis), array.shape[dim])
        up = [(i, (i + 1) % devices) for i in range(devices)]
        down = [(j, i) for i, j in up]
        last = lax.slice_in_dim(array, length - width, length, axis=dim)
        leading = lax.slice_in_dim(array, 0, width, axis=dim)
        before = lax.ppermute(last, axis, up)
        after = lax.ppermute(leading, axis, down)
        array = jnp.concatenate([before, array, after], axis=dim)
    return array


def add_partners(local):
    face = local.shape[0] // 4
    columns = local.shape[1]
    faces = local.reshape(4, face, columns)
    along_sub = extended(faces[0:2], (("sub", 0),), 1)
    along_grp = extended(faces[2:4], (("grp", 0),), 1)
    summed = jnp.stack(
        [
            faces[0] + along_sub[0],
            faces[1] + along_sub[3],
            faces[2] + along_grp[0],
            faces[3] + along_grp[3],
        ]
    )
    return summed.reshape(4 * face, columns)


def shards(
    schur_t, neumann_t, face_weights, coarse_basis, coarse_inverse, coarse_number, loads, iterate
):
    schur = schur_t[0, 0]
    neumann = neumann_t[0, 0]
    weights = face_weights[0, 0][:, None]
    basis = coarse_basis[0, 0]
    basis_wide = basis.astype(jnp.float32)
    basis_across = basis.T
    inverse_rows = coarse_inverse[0]
    numbers = coarse_number[0]
    per_sub = basis.shape[1]
    coarse_order = inverse_rows.shape[1]
    highest = lax.Precision.HIGHEST
    own = lax.dynamic_slice_in_dim(numbers, lax.axis_index("sub") * per_sub, per_sub)
    load_wide = loads[0, 0].astype(jnp.float32)
    current = iterate[0, 0]
    for step in range(ITERS):
        image = jnp.dot(schur, current, preferred_element_type=jnp.float32)
        resid = add_partners(load_wide - image)
        weighted = (weights * resid).astype(jnp.bfloat16)
        local_coarse = jnp.dot(basis_across, weighted, preferred_element_type=jnp.float32)
        scattered = jax.ops.segment_sum(local_coarse, own, num_segments=coarse_order)
        coarse_rhs = lax.psum(scattered, "sub")
        solved_rows = jnp.dot(inverse_rows, coarse_rhs, precision=highest)
        solved = lax.all_gather(solved_rows, "sub", axis=0, tiled=True)
        own_values = jnp.take(solved, own, axis=0)
        fine = jnp.dot(neumann, weighted, preferred_element_type=jnp.float32)
        correction = fine + jnp.dot(basis_wide, own_values, precision=highest)
        update = add_partners(weights * correction)
        current = (current.astype(jnp.float32) + update).astype(jnp.bfloat16)
    return current[None, None]


def solution(mesh):
    return jax.shard_map(
        shards,
        mesh=mesh,
        in_specs=(
            P("grp", "sub", None, None),
            P("grp", "sub", None, None),
            P("grp", "sub", None),
            P("grp", "sub", None, None),
            P("grp", "sub", None),
            P("grp", None),
            P("grp", "sub", None, None),
            P("grp", "sub", None, None),
        ),
        out_specs=P("grp", "sub", None, None),
        check_vma=False,
    )
```

profile of v0, /device:TPU:241, one launch (start us, length us, event | category | flops | bytes accessed | tf_op | source)
XLA Modules:
  0.0 2029.4 jit_solution(9209375182098139773)
XLA Ops:
  10.6 5.1 collective-permute-start
  18.8 4.3 collective-permute-start.3
  27.5 7.6 collective-permute-done.1
  41.2 531.6 %all-reduce.4.cloned.1.call-done = f32[768,128]{1,0:T(8,128)} async-done(((f32[768,128]{1,0:T(8,128)}), f32[768,128]{1,0:T(8,128)}) %all-reduce.4.cloned.1.call-update) | async-done | bytes 393232 | tf_op jit(solution)/shard_map/psum | solution.py:62
  574.1 76.8 %all-gather = f32[64,12,128]{2,1,0:T(8,128)S(1)} all-gather(f32[1,12,128]{2,1,0:T(8,128)S(1)} %convolution_bitcast_fusion.5), channel_id=1, replica_groups=mesh['grp'=8,'sub'=64] {'sub'}, dimensions={0}, use_global_device_ids=true | all-gather | bytes 399360 | tf_op jit(solution)/shard_map/all_gather | solution.py:64
  653.9 7.6 collective-permute-start.4
  664.6 4.3 collective-permute-start.7
  672.5 8.6 collective-permute-done.5
  689.0 5.5 collective-permute-start.11
  697.5 7.7 collective-permute-done.9
  707.1 3.2 fusion.2
  710.3 531.1 %all-reduce.6.cloned.1.call-done = f32[768,128]{1,0:T(8,128)} async-done(((f32[768,128]{1,0:T(8,128)}), f32[768,128]{1,0:T(8,128)}) %all-reduce.6.cloned.1.call-update) | async-done | bytes 393232 | tf_op jit(solution)/shard_map/psum | solution.py:62
  1242.8 76.8 %all-gather.1 = f32[64,12,128]{2,1,0:T(8,128)S(1)} all-gather(f32[1,12,128]{2,1,0:T(8,128)S(1)} %convolution_bitcast_fusion.4), channel_id=1, replica_groups=mesh['grp'=8,'sub'=64] {'sub'}, dimensions={0}, use_global_device_ids=true | all-gather | bytes 399360 | tf_op jit(solution)/shard_map/all_gather | solution.py:64
  1323.6 7.6 collective-permute-start.12
  1334.3 4.3 collective-permute-start.15
  1340.5 9.9 collective-permute-done.13
  1356.2 5.5 collective-permute-start.19
  1364.7 7.7 collective-permute-done.17
  1374.2 3.2 fusion
  1377.5 531.1 %all-reduce.8.cloned.1.call-done = f32[768,128]{1,0:T(8,128)} async-done(((f32[768,128]{1,0:T(8,128)}), f32[768,128]{1,0:T(8,128)}) %all-reduce.8.cloned.1.call-update) | async-done | bytes 393232 | tf_op jit(solution)/shard_map/psum | solution.py:62
  1909.9 76.8 %all-gather.2 = f32[64,12,128]{2,1,0:T(8,128)S(1)} all-gather(f32[1,12,128]{2,1,0:T(8,128)S(1)} %convolution_bitcast_fusion.3), channel_id=1, replica_groups=mesh['grp'=8,'sub'=64] {'sub'}, dimensions={0}, use_global_device_ids=true | all-gather | bytes 399360 | tf_op jit(solution)/shard_map/all_gather | solution.py:64
  1991.4 7.6 collective-permute-start.20
  2002.2 4.3 collective-permute-start.23
  2011.5 7.2 collective-permute-done.21
  (113 shorter events, 80.2 us)
Async XLA Ops:
  6.5 566.2 %all-reduce.4.cloned.1.call-start = ((), (), s32[]{:S(2)}) async-start(), calls=%async_computation | async-start | bytes 786432 | tf_op jit(solution)/shard_map/psum | solution.py:62
  10.6 16.3 collective-permute-start
  15.6 11.2 collective-permute-start.2
  23.1 12.0 collective-permute-start.1
  37.9 1203.5 %all-reduce.6.cloned.1.call-start = ((), (), s32[]{:S(2)}) async-start(), calls=%async_computation.1 | async-start | bytes 786432 | tf_op jit(solution)/shard_map/psum | solution.py:62
  653.9 17.9 collective-permute-start.4
  661.5 10.3 collective-permute-start.6
  668.9 12.2 collective-permute-start.5
  685.1 12.3 collective-permute-start.8
  687.1 10.4 collective-permute-start.10
  689.0 8.5 collective-permute-start.11
  694.5 10.7 collective-permute-start.9
  707.1 1201.5 %all-reduce.8.cloned.1.call-start = ((), (), s32[]{:S(2)}) async-start(), calls=%async_computation.2 | async-start | bytes 786432 | tf_op jit(solution)/shard_map/psum | solution.py:62
  1323.6 17.0 collective-permute-start.12
  1331.2 9.3 collective-permute-start.14
  1338.6 11.9 collective-permute-start.13
  1352.4 12.3 collective-permute-start.16
  1354.3 10.4 collective-permute-start.18
  1356.2 8.5 collective-permute-start.19
  1361.7 10.7 collective-permute-start.17
  1991.4 20.0 collective-permute-start.20
  1999.1 12.4 collective-permute-start.22
  2002.2 9.3 collective-permute-start.23
  2006.5 12.2 collective-permute-start.21
  (14 other events, 1889.6 us)
Sparse Core Ops, SparseCore 0:
  38.0 534.7 all-reduce.3
  707.2 534.2 all-reduce.5
  1374.4 534.2 all-reduce.7
where the time goes:
time: 2030 us
  waiting for transfers between devices  1640 us (81%)
  blocking collectives  231 us (11%)
  starting transfers between devices  89.8 us (4%)
  matrix products  21.8 us (1%)
    psum x3, waiting for transfers between devices, shards(): coarse_rhs = lax.psum(scattered, 'sub')  1590 us
    all_gather x3, blocking collectives, shards(): solved = lax.all_gather(solved_rows, 'sub', axis=0, tiled=True)  231 us
    ppermute x12, waiting for transfers between devices, extended(): after = lax.ppermute(leading, axis, down)  48.7 us
    ppermute x12, starting transfers between devices, extended(): before = lax.ppermute(last, axis, up)  48 us
    ppermute x12, starting transfers between devices, extended(): after = lax.ppermute(leading, axis, down)  41.7 us
  transfers between devices with their start and end apart: 27, of which 9 were waited for; matrix products, arithmetic and copies ran while one was open for 1% of the time, Pallas kernels for 0%

commit v1 on v0

--- a/solution.py
+++ b/solution.py
@@ -4,6 +4,11 @@
 from jax.sharding import PartitionSpec as P
 
 ITERS = 3
+
+
+def add_all(shard, axis):
+    parts = lax.all_gather(shard, axis)
+    return jnp.sum(parts, axis=0)
 
 
 def extended(array, sides, width):
@@ -59,7 +64,7 @@
         weighted = (weights * resid).astype(jnp.bfloat16)
         local_coarse = jnp.dot(basis_across, weighted, preferred_element_type=jnp.float32)
         scattered = jax.ops.segment_sum(local_coarse, own, num_segments=coarse_order)
-        coarse_rhs = lax.psum(scattered, "sub")
+        coarse_rhs = add_all(scattered, "sub")
         solved_rows = jnp.dot(inverse_rows, coarse_rhs, precision=highest)
         solved = lax.all_gather(solved_rows, "sub", axis=0, tiled=True)
         own_values = jnp.take(solved, own, axis=0)

time: 2030 us -> 988 us (0.49)
  the two profiles are of different devices: /device:TPU:241 before, /device:TPU:14 now
where the time goes in v1:
time: 988 us; the launch traced here: 986 us
  waiting for transfers between devices  538 us (54%)
  blocking collectives  253 us (26%)
  starting transfers between devices  99.9 us (10%)
  other arithmetic  42.3 us (4%)
  matrix products  19.9 us (2%)
  local copies, waits for them, and re-layouts  19.5 us (2%)
  between operations  13.6 us (1%)
    all_gather x3, waiting for transfers between devices, add_all(): parts = lax.all_gather(shard, axis)  510 us
    all_gather x3, blocking collectives, shards(): solved = lax.all_gather(solved_rows, 'sub', axis=0, tiled=True)  253 us
    ppermute x12, starting transfers between devices, extended(): after = lax.ppermute(leading, axis, down)  67.8 us
    ppermute x12, starting transfers between devices, extended(): before = lax.ppermute(last, axis, up)  32.1 us
    reduce_sum x3, other arithmetic, add_all(): return jnp.sum(parts, axis=0)  27.9 us
    ppermute x12, waiting for transfers between devices, extended(): after = lax.ppermute(leading, axis, down)  24.5 us
  transfers between devices with their start and end apart: 27, of which 13 were waited for; matrix products, arithmetic and copies ran while one was open for 2% of the time, Pallas kernels for 0%

profile of v1, /device:TPU:14, one launch (start us, length us, event | category | flops | bytes accessed | tf_op | source)
XLA Modules:
  0.0 986.0 jit_solution(6942206534197960391)
XLA Ops:
  12.5 13.2 %collective-permute-start.1 = (f32[1,256,128]{2,1,0:T(8,128)S(1)}, f32[1,256,128]{2,1,0:T(8,128)S(1)}, u32[]{:S(2)}, u32[]{:S(2)}) collective-permute-start(f32[1,256,128]{2,1,0:T(8,128)S(1)} %get-tuple-element.59), channel_id=1, source_target_pairs={{1,0},{2,1},{3,2},{4,3},{5,4},{6,5},{7,6},{8,7},{9,8},{10,9},{11,1... | collective-permute-start | bytes 393224 | tf_op jit(solution)/shard_map/ppermute | solution.py:22
  34.1 3.8 collective-permute-done.3
  44.1 169.8 %all-gather.10.cloned.1.call-done = f32[49152,128]{1,0:T(8,128)} async-done(((f32[768,128]{1,0:T(8,128)}), f32[49152,128]{1,0:T(8,128)}) %all-gather.10.cloned.1.call-update) | async-done | bytes 25165840 | tf_op jit(solution)/shard_map/all_gather | solution.py:10
  213.9 9.0 reduce_sum.27
  223.3 82.5 %all-gather.3 = f32[64,12,128]{2,1,0:T(8,128)S(1)} all-gather(f32[1,12,128]{2,1,0:T(8,128)S(1)} %convolution_bitcast_fusion.5), channel_id=1, replica_groups=mesh['grp'=8,'sub'=64] {'sub'}, dimensions={0}, use_global_device_ids=true | all-gather | bytes 399360 | tf_op jit(solution)/shard_map/all_gather | solution.py:69
  312.7 7.5 collective-permute-start.5
  320.2 4.2 collective-permute-start.6
  327.4 6.3 collective-permute-done.7
  339.5 3.9 collective-permute-start.11
  345.4 7.9 collective-permute-start.9
  361.0 171.5 %all-gather.12.cloned.1.call-done = f32[49152,128]{1,0:T(8,128)} async-done(((f32[768,128]{1,0:T(8,128)}), f32[49152,128]{1,0:T(8,128)}) %all-gather.12.cloned.1.call-update) | async-done | bytes 25165840 | tf_op jit(solution)/shard_map/all_gather | solution.py:10
  532.4 9.8 reduce_sum.28
  543.5 87.7 %all-gather.4 = f32[64,12,128]{2,1,0:T(8,128)} all-gather(f32[1,12,128]{2,1,0:T(8,128)S(1)} %convolution_bitcast_fusion.4), channel_id=1, replica_groups=mesh['grp'=8,'sub'=64] {'sub'}, dimensions={0}, use_global_device_ids=true | all-gather | bytes 399360 | tf_op jit(solution)/shard_map/all_gather | solution.py:69
  638.5 7.5 collective-permute-start.13
  646.0 4.2 collective-permute-start.14
  652.9 6.3 collective-permute-done.15
  663.0 7.9 collective-permute-start.17
  672.8 3.9 collective-permute-start.19
  677.8 4.0 collective-permute-done.19
  686.9 168.9 %all-gather.14.cloned.1.call-done = f32[49152,128]{1,0:T(8,128)} async-done(((f32[768,128]{1,0:T(8,128)}), f32[49152,128]{1,0:T(8,128)}) %all-gather.14.cloned.1.call-update) | async-done | bytes 25165840 | tf_op jit(solution)/shard_map/all_gather | solution.py:10
  855.8 9.0 reduce_sum.29
  865.1 82.5 %all-gather.5 = f32[64,12,128]{2,1,0:T(8,128)S(1)} all-gather(f32[1,12,128]{2,1,0:T(8,128)S(1)} %convolution_bitcast_fusion.3), channel_id=1, replica_groups=mesh['grp'=8,'sub'=64] {'sub'}, dimensions={0}, use_global_device_ids=true | all-gather | bytes 399360 | tf_op jit(solution)/shard_map/all_gather | solution.py:69
  954.5 7.5 collective-permute-start.21
  962.0 4.2 collective-permute-start.22
  (108 shorter events, 89.3 us)
Async XLA Ops:
  6.5 207.3 %all-gather.10.cloned.1.call-start = ((), (), s32[]{:S(2)}) async-start(), calls=%async_computation | async-start | bytes 25559040 | tf_op jit(solution)/shard_map/all_gather | solution.py:10
  10.6 22.9 %collective-permute-start = (f32[1,256,128]{2,1,0:T(8,128)}, f32[1,256,128]{2,1,0:T(8,128)S(1)}, u32[]{:S(2)}, u32[]{:S(2)}) collective-permute-start(f32[1,256,128]{2,1,0:T(8,128)} %get-tuple-element.56), channel_id=1, source_target_pairs={{0,1},{1,2},{2,3},{3,4},{4,5},{5,6},{6,7},{7,8},{8,9},{9,10},{10,1... | collective-permute-start | bytes 393224 | tf_op jit(solution)/shard_map/ppermute | solution.py:21
  12.5 21.0 %collective-permute-start.1 = (f32[1,256,128]{2,1,0:T(8,128)S(1)}, f32[1,256,128]{2,1,0:T(8,128)S(1)}, u32[]{:S(2)}, u32[]{:S(2)}) collective-permute-start(f32[1,256,128]{2,1,0:T(8,128)S(1)} %get-tuple-element.59), channel_id=1, source_target_pairs={{1,0},{2,1},{3,2},{4,3},{5,4},{6,5},{7,6},{8,7},{9,8},{10,9},{11,1... | collective-permute-start | bytes 393224 | tf_op jit(solution)/shard_map/ppermute | solution.py:22
  25.7 7.8 collective-permute-start.2
  28.9 9.1 collective-permute-start.3
  40.8 491.7 %all-gather.12.cloned.1.call-start = ((), (), s32[]{:S(2)}) async-start(), calls=%async_computation.1 | async-start | bytes 25559040 | tf_op jit(solution)/shard_map/all_gather | solution.py:10
  310.4 16.9 %collective-permute-start.4 = (f32[1,256,128]{1,2,0:T(8,128)}, f32[1,256,128]{1,2,0:T(8,128)S(1)}, u32[]{:S(2)}, u32[]{:S(2)}) collective-permute-start(f32[1,256,128]{1,2,0:T(8,128)} %get-tuple-element.48), channel_id=1, source_target_pairs={{0,1},{1,2},{2,3},{3,4},{4,5},{5,6},{6,7},{7,8},{8,9},{9,10},{10,1... | collective-permute-start | bytes 393224 | tf_op jit(solution)/shard_map/ppermute | solution.py:21
  312.7 14.6 %collective-permute-start.5 = (f32[1,256,128]{1,2,0:T(8,128)}, f32[1,256,128]{1,2,0:T(8,128)S(1)}, u32[]{:S(2)}, u32[]{:S(2)}) collective-permute-start(f32[1,256,128]{1,2,0:T(8,128)} %get-tuple-element.51), channel_id=1, source_target_pairs={{1,0},{2,1},{3,2},{4,3},{5,4},{6,5},{7,6},{8,7},{9,8},{10,9},{11,1... | collective-permute-start | bytes 393224 | tf_op jit(solution)/shard_map/ppermute | solution.py:22
  324.4 9.3 collective-permute-start.7
  337.6 15.7 %collective-permute-start.10 = (f32[1,256,128]{2,1,0:T(8,128)S(1)}, f32[1,256,128]{2,1,0:T(8,128)S(1)}, u32[]{:S(2)}, u32[]{:S(2)}) collective-permute-start(f32[1,256,128]{2,1,0:T(8,128)S(1)} %get-tuple-element.41), channel_id=1, source_target_pairs={{0,64},{64,128},{128,192},{192,256},{256,320},{320,384},{384,448},... | collective-permute-start | bytes 393224 | tf_op jit(solution)/shard_map/ppermute | solution.py:21
  339.5 13.7 %collective-permute-start.11 = (f32[1,256,128]{2,1,0:T(8,128)S(1)}, f32[1,256,128]{2,1,0:T(8,128)S(1)}, u32[]{:S(2)}, u32[]{:S(2)}) collective-permute-start(f32[1,256,128]{2,1,0:T(8,128)S(1)} %get-tuple-element.42), channel_id=1, source_target_pairs={{64,0},{128,64},{192,128},{256,192},{320,256},{384,320},{448,384},... | collective-permute-start | bytes 393224 | tf_op jit(solution)/shard_map/ppermute | solution.py:22
  343.5 11.4 %collective-permute-start.8 = (f32[1,256,128]{2,1,0:T(8,128)S(1)}, f32[1,256,128]{2,1,0:T(8,128)S(1)}, u32[]{:S(2)}, u32[]{:S(2)}) collective-permute-start(f32[1,256,128]{2,1,0:T(8,128)S(1)} %get-tuple-element.40), channel_id=1, source_target_pairs={{0,1},{1,2},{2,3},{3,4},{4,5},{5,6},{6,7},{7,8},{8,9},{9,10},{10,1... | collective-permute-start | bytes 393224 | tf_op jit(solution)/shard_map/ppermute | solution.py:21
  345.4 10.4 %collective-permute-start.9 = (f32[1,256,128]{2,1,0:T(8,128)S(1)}, f32[1,256,128]{2,1,0:T(8,128)S(1)}, u32[]{:S(2)}, u32[]{:S(2)}) collective-permute-start(f32[1,256,128]{2,1,0:T(8,128)S(1)} %get-tuple-element.43), channel_id=1, source_target_pairs={{1,0},{2,1},{3,2},{4,3},{5,4},{6,5},{7,6},{8,7},{9,8},{10,9},{11,1... | collective-permute-start | bytes 393224 | tf_op jit(solution)/shard_map/ppermute | solution.py:22
  357.6 498.1 %all-gather.14.cloned.1.call-start = ((), (), s32[]{:S(2)}) async-start(), calls=%async_computation.2 | async-start | bytes 25559040 | tf_op jit(solution)/shard_map/all_gather | solution.py:10
  636.2 15.9 %collective-permute-start.12 = (f32[1,256,128]{1,2,0:T(8,128)S(1)}, f32[1,256,128]{1,2,0:T(8,128)S(1)}, u32[]{:S(2)}, u32[]{:S(2)}) collective-permute-start(f32[1,256,128]{1,2,0:T(8,128)S(1)} %get-tuple-element.32), channel_id=1, source_target_pairs={{0,1},{1,2},{2,3},{3,4},{4,5},{5,6},{6,7},{7,8},{8,9},{9,10},{10,1... | collective-permute-start | bytes 393224 | tf_op jit(solution)/shard_map/ppermute | solution.py:21
  638.5 13.7 %collective-permute-start.13 = (f32[1,256,128]{1,2,0:T(8,128)S(1)}, f32[1,256,128]{1,2,0:T(8,128)S(1)}, u32[]{:S(2)}, u32[]{:S(2)}) collective-permute-start(f32[1,256,128]{1,2,0:T(8,128)S(1)} %get-tuple-element.35), channel_id=1, source_target_pairs={{1,0},{2,1},{3,2},{4,3},{5,4},{6,5},{7,6},{8,7},{9,8},{10,9},{11,1... | collective-permute-start | bytes 393224 | tf_op jit(solution)/shard_map/ppermute | solution.py:22
  650.2 9.0 collective-permute-start.15
  661.1 15.7 %collective-permute-start.16 = (f32[1,256,128]{2,1,0:T(8,128)S(1)}, f32[1,256,128]{2,1,0:T(8,128)S(1)}, u32[]{:S(2)}, u32[]{:S(2)}) collective-permute-start(f32[1,256,128]{2,1,0:T(8,128)S(1)} %get-tuple-element.24), channel_id=1, source_target_pairs={{0,1},{1,2},{2,3},{3,4},{4,5},{5,6},{6,7},{7,8},{8,9},{9,10},{10,1... | collective-permute-start | bytes 393224 | tf_op jit(solution)/shard_map/ppermute | solution.py:21
  663.0 13.7 %collective-permute-start.17 = (f32[1,256,128]{2,1,0:T(8,128)S(1)}, f32[1,256,128]{2,1,0:T(8,128)S(1)}, u32[]{:S(2)}, u32[]{:S(2)}) collective-permute-start(f32[1,256,128]{2,1,0:T(8,128)S(1)} %get-tuple-element.27), channel_id=1, source_target_pairs={{1,0},{2,1},{3,2},{4,3},{5,4},{6,5},{7,6},{8,7},{9,8},{10,9},{11,1... | collective-permute-start | bytes 393224 | tf_op jit(solution)/shard_map/ppermute | solution.py:22
  672.8 9.0 collective-permute-start.19
  952.3 20.0 %collective-permute-start.20 = (f32[1,256,128]{1,2,0:T(8,128)}, f32[1,256,128]{1,2,0:T(8,128)S(1)}, u32[]{:S(2)}, u32[]{:S(2)}) collective-permute-start(f32[1,256,128]{1,2,0:T(8,128)} %get-tuple-element.16), channel_id=1, source_target_pairs={{0,1},{1,2},{2,3},{3,4},{4,5},{5,6},{6,7},{7,8},{8,9},{9,10},{10,1... | collective-permute-start | bytes 393224 | tf_op jit(solution)/shard_map/ppermute | solution.py:21
  954.5 17.8 %collective-permute-start.21 = (f32[1,256,128]{1,2,0:T(8,128)}, f32[1,256,128]{1,2,0:T(8,128)S(1)}, u32[]{:S(2)}, u32[]{:S(2)}) collective-permute-start(f32[1,256,128]{1,2,0:T(8,128)} %get-tuple-element.19), channel_id=1, source_target_pairs={{1,0},{2,1},{3,2},{4,3},{5,4},{6,5},{7,6},{8,7},{9,8},{10,9},{11,1... | collective-permute-start | bytes 393224 | tf_op jit(solution)/shard_map/ppermute | solution.py:22
  962.0 10.2 %collective-permute-start.22 = (f32[1,256,128]{1,2,0:T(8,128)S(1)}, f32[1,256,128]{1,2,0:T(8,128)S(1)}, u32[]{:S(2)}, u32[]{:S(2)}) collective-permute-start(f32[1,256,128]{1,2,0:T(8,128)S(1)} %get-tuple-element.17), channel_id=1, source_target_pairs={{0,64},{64,128},{128,192},{192,256},{256,320},{320,384},{384,448},... | collective-permute-start | bytes 393224 | tf_op jit(solution)/shard_map/ppermute | solution.py:21
  966.2 9.1 collective-permute-start.23
  (10 other events, 200.0 us)
Sparse Core Ops, SparseCore 0:
  40.9 172.9 all-gather.9
  357.7 174.6 all-gather.11
  683.8 171.8 all-gather.13
